TPU v7x, 512 devices: a whole 4x8x8 slice. The times are simulated.
512 devices in a mesh: ctx: 64 (over x, y_lo, z), tp: 8 (over y_hi, core).
Axes of the slice: x: 4, y: 8 (y_hi: 4, y_lo: 2; y = y_hi * 2 + y_lo), z: 8, core: 2. Of those that a mesh axis runs over, the one named last changes fastest.
Arguments:
- query_vectors: bfloat16 [8192, 3072], P(('ctx', 'tp')), may hold values from -20 to 20
- key_vectors: bfloat16 [8192, 3072], P(('ctx', 'tp')), may hold values from -20 to 20
- value_vectors: bfloat16 [8192, 3072], P(('ctx', 'tp')), may hold values from -6 to 6
- out_weight: bfloat16 [3072, 5120], P('tp'), may hold values from -0.109375 to 0.109375
Outputs:
- mixed: bfloat16 [8192, 5120], P(('ctx', 'tp'))
All inputs are finite; a program needn't handle non-finite values.
Results may differ from a plain program's by a relative error of at most 0.027.
Values may be sent and summed in bfloat16 or wider, within the bound.
A program may use at most 64 MiB of HBM per device.

v0:
```python
import math
import jax
import jax.numpy as jnp
from jax import lax
from jax.sharding import PartitionSpec as P

HD = 128


def fresh_state(row_count, head_count):
    row_peak = jnp.full((row_count, head_count), -1e30, jnp.float32)
    row_total = jnp.zeros((row_count, head_count), jnp.float32)
    weighted = jnp.zeros((row_count, head_count, HD), jnp.float32)
    return (row_peak, row_total, weighted)


def attend_piece(running, query_heads, key_rows, value_rows, score_scale):
    head_count = query_heads.shape[1]
    piece_rows = key_rows.shape[0]
    sub_rows = math.gcd(piece_rows, 256)
    sub_count = piece_rows // sub_rows
    key_parts = key_rows.reshape(sub_count, sub_rows, head_count, HD)
    value_parts = value_rows.reshape(sub_count, sub_rows, head_count, HD)

    def absorb(current, part_pair):
        row_peak, row_total, weighted = current
        key_part, value_part = part_pair
        scores = (
            jnp.einsum("ihd,jhd->ihj", query_heads, key_part, preferred_element_type=jnp.float32)
            * score_scale
        )
        new_peak = jnp.maximum(row_peak, jnp.max(scores, axis=-1))
        weights_low = jnp.exp(scores - new_peak[..., None]).astype(jnp.bfloat16)
        shrink = jnp.exp(row_peak - new_peak)
        row_total = row_total * shrink + jnp.sum(weights_low.astype(jnp.float32), axis=-1)
        weighted = weighted * shrink[..., None] + jnp.einsum(
            "ihj,jhd->ihd", weights_low, value_part, preferred_element_type=jnp.float32
        )
        return ((new_peak, row_total, weighted), None)

    finished, unused = lax.scan(absorb, running, (key_parts, value_parts))
    return finished


def local(query_vectors, key_vectors, value_vectors, out_weight):
    score_scale = 1.0 / math.sqrt(HD)
    tp_count = lax.axis_size("tp")
    all_queries = lax.all_gather(query_vectors, "tp", axis=0, tiled=True)
    row_count = all_queries.shape[0]
    head_count = all_queries.shape[1] // HD
    query_heads = all_queries.reshape(row_count, head_count, HD)
    row_peak, row_total, weighted = attend_piece(
        fresh_state(row_count, head_count),
        query_heads,
        lax.all_gather(key_vectors, "ctx", axis=0, tiled=True),
        lax.all_gather(value_vectors, "ctx", axis=0, tiled=True),
        score_scale,
    )
    top_peak = lax.pmax(row_peak, "tp")
    factor = jnp.exp(row_peak - top_peak)
    all_totals = lax.psum(row_total * factor, "tp")
    numerator = (weighted * factor[..., None]).reshape(row_count, head_count * HD)
    own_numerator = lax.psum_scatter(
        numerator.astype(jnp.bfloat16), "tp", scatter_dimension=1, tiled=True
    ).astype(jnp.float32)
    own_heads = head_count // tp_count
    own_totals = lax.dynamic_slice_in_dim(
        all_totals, lax.axis_index("tp") * own_heads, own_heads, 1
    )
    attended = (own_numerator.reshape(row_count, own_heads, HD) / own_totals[..., None]).astype(
        jnp.bfloat16
    )
    attended = attended.reshape(row_count, own_heads * HD)
    return lax.psum_scatter(
        jnp.dot(attended, out_weight, preferred_element_type=jnp.float32).astype(jnp.bfloat16),
        "tp",
        scatter_dimension=0,
        tiled=True,
    )


def solution(mesh):
    return jax.shard_map(
        local,
        mesh=mesh,
        in_specs=(
            P(("ctx", "tp"), None),
            P(("ctx", "tp"), None),
            P(("ctx", "tp"), None),
            P("tp", None),
        ),
        out_specs=P(("ctx", "tp"), None),
        check_vma=False,
    )
```

profile of v0, /device:TPU:21, one launch (start us, length us, event | category | flops | bytes accessed | tf_op | source)
XLA Modules:
  0.0 811.8 jit_solution(7666811695530442042)
XLA Ops:
  6.5 0.7 all-gather.5.cloned.1.call-update
  7.3 0.7 all-gather.3.cloned.1.call-update
  8.1 17.3 %all_gather.10 = bf16[128,3072]{1,0:T(8,128)(2,1)S(1)} all-gather(bf16[16,3072]{1,0:T(8,128)(2,1)} %param.6), channel_id=1, replica_groups=mesh['ctx'=64,'tp'=8] {'tp'}, dimensions={0}, use_global_device_ids=true | all-gather | bytes 884736 | tf_op jit(solution)/shard_map/all_gather | solution.py:48
  25.8 1.2 copy.14
  27.0 224.2 %all-gather.5.cloned.1.call-done = bf16[1024,3072]{1,0:T(8,128)(2,1)} async-done(((bf16[16,3072]{1,0:T(8,128)(2,1)}), bf16[1024,3072]{1,0:T(8,128)(2,1)}) %all-gather.5.cloned.1.call-update) | async-done | bytes 6291472 | tf_op jit(solution)/shard_map/all_gather | solution.py:56
  251.1 7.4 copy.20
  258.5 303.4 %all-gather.3.cloned.1.call-done = bf16[1024,3072]{1,0:T(8,128)(2,1)} async-done(((bf16[16,3072]{1,0:T(8,128)(2,1)}), bf16[1024,3072]{1,0:T(8,128)(2,1)}) %all-gather.3.cloned.1.call-update) | async-done | bytes 6291472 | tf_op jit(solution)/shard_map/all_gather | solution.py:55
  562.0 7.4 copy.19
  569.4 46.2 %while.15 = (s32[]{:T(128)}, f32[128,24]{0,1:T(8,128)S(1)}, f32[128,24]{0,1:T(8,128)S(1)}, f32[128,24,128]{0,2,1:T(8,128)}, bf16[4,256,24,128]{3,2,1,0:T(8,128)(...) while((s32[]{:T(128)}, f32[128,24]{0,1:T(8,128)S(1)}, ...), condition=%wide.region_3.4_spmd.clone, body=%wide.region_0.3_spmd.clone.sunk | while | flops 411712512 | bytes 29294728 | solution.py:41
  569.4 3.6 constant_dynamic-slice_fusion.4
  573.0 0.6 bitcast_reduce_fusion.2
  574.2 2.9 copy.28
  577.1 3.5 bitcast_add_fusion.2
  580.6 3.6 constant_dynamic-slice_fusion.4
  584.2 0.6 bitcast_reduce_fusion.2
  585.4 2.9 copy.28
  588.3 4.0 bitcast_add_fusion.2
  592.2 3.6 constant_dynamic-slice_fusion.4
  595.9 0.6 bitcast_reduce_fusion.2
  597.1 2.9 copy.28
  599.9 3.9 bitcast_add_fusion.2
  603.9 3.6 constant_dynamic-slice_fusion.4
  607.5 0.6 bitcast_reduce_fusion.2
  608.7 2.9 copy.28
  611.6 3.9 bitcast_add_fusion.2
  615.6 66.1 %pmax.7 = f32[128,24]{0,1:T(8,128)S(1)} all-reduce(f32[128,24]{0,1:T(8,128)S(1)} %get-tuple-element.45), channel_id=1, replica_groups=mesh['ctx'=64,'tp'=8] {'tp'}, use_global_device_ids=true, to_apply=%region_4.5 | all-reduce | flops 3072 | bytes 24576 | tf_op jit(solution)/shard_map/pmax | solution.py:59
  681.7 2.5 multiply_convert_fusion
  684.3 27.2 %psum.7 = f32[128,24]{0,1:T(8,128)S(1)} all-reduce(f32[128,24]{0,1:T(8,128)S(1)} %get-tuple-element.101), channel_id=1, replica_groups=mesh['ctx'=64,'tp'=8] {'tp'}, use_global_device_ids=true, to_apply=%region_6.7 | all-reduce | flops 3072 | bytes 24576 | tf_op jit(solution)/shard_map/psum | solution.py:61
  711.5 46.7 %reduce-scatter.3.cloned.1.call-done = bf16[128,384]{0,1:T(8,128)(2,1)} async-done(((bf16[128,3072]{0,1:T(8,128)(2,1)}), bf16[128,384]{0,1:T(8,128)(2,1)}) %reduce-scatter.3.cloned.1.call-update) | async-done | bytes 98320 | tf_op jit(solution)/shard_map/reduce_scatter | solution.py:63
  758.2 0.9 fusion.10
  759.1 4.1 convolution_convert_fusion
  763.2 42.1 %reduce-scatter.5.cloned.1.call-done = bf16[16,5120]{1,0:T(8,128)(2,1)} async-done(((bf16[128,5120]{1,0:T(8,128)(2,1)}), bf16[16,5120]{1,0:T(8,128)(2,1)}) %reduce-scatter.5.cloned.1.call-update) | async-done | bytes 163856 | tf_op jit(solution)/shard_map/reduce_scatter | solution.py:74
  (36 shorter events, 2.8 us)
Async XLA Ops:
  6.5 244.6 %all-gather.5.cloned.1.call-start = ((), (), s32[]{:S(2)}) async-start(), calls=%async_computation.3 | async-start | bytes 6389760 | tf_op jit(solution)/shard_map/all_gather | solution.py:56
  7.3 554.7 %all-gather.3.cloned.1.call-start = ((), (), s32[]{:S(2)}) async-start(), calls=%async_computation.2 | async-start | bytes 6389760 | tf_op jit(solution)/shard_map/all_gather | solution.py:55
  8.0 750.2 %reduce-scatter.3.cloned.1.call-start = ((), (), s32[]{:S(2)}) async-start(), calls=%async_computation.4 | async-start | bytes 884736 | tf_op jit(solution)/shard_map/reduce_scatter | solution.py:63
  569.4 3.6 copy-start
  580.6 3.6 copy-start
  592.2 3.6 copy-start
  603.9 3.6 copy-start
  684.2 121.1 %reduce-scatter.5.cloned.1.call-start = ((), (), s32[]{:S(2)}) async-start(), calls=%async_computation.5 | async-start | bytes 1474560 | tf_op jit(solution)/shard_map/reduce_scatter | solution.py:74
Sparse Core Ops, SparseCore 0:
  9.4 241.6 all-gather.4
  253.2 308.6 all-gather.2
  684.3 73.7 reduce-scatter.2
  763.3 41.9 reduce-scatter.4
where the time goes:
time: 812 us
  waiting for transfers between devices  618 us (76%)
  blocking collectives  111 us (14%)
  local copies, waits for them, and re-layouts  42.5 us (5%)
  matrix products  21.7 us (3%)
  between operations  13.2 us (2%)
    all_gather x1, waiting for transfers between devices, local(): lax.all_gather(key_vectors, 'ctx', axis=0, tiled=True)  303 us
    all_gather x1, waiting for transfers between devices, local(): lax.all_gather(value_vectors, 'ctx', axis=0, tiled=True)  224 us
    pmax x1, blocking collectives, local(): top_peak = lax.pmax(row_peak, 'tp')  66.1 us
    reduce_scatter x1, waiting for transfers between devices, local(): lax.psum_scatter(numerator.astype(jnp.bfloat16), 'tp', scatter_dimension=...  46.7 us
    reduce_scatter x1, waiting for transfers between devices, local(): lax.psum_scatter(jnp.dot(attended, out_weight, preferred_element_type=jnp...  42.1 us
    psum x1, blocking collectives, local(): all_totals = lax.psum(row_total * factor, 'tp')  27.2 us
    dynamic_slice x8, local copies, waits for them, and re-layouts, attend_piece(): finished, unused = lax.scan(absorb, running, (key_parts, value_parts))  26.1 us
    all_gather x1, blocking collectives, local(): all_queries = lax.all_gather(query_vectors, 'tp', axis=0, tiled=True)  17.3 us
  transfers between devices with their start and end apart: 4, of which 4 were waited for; matrix products, arithmetic and copies ran while one was open for 1% of the time, Pallas kernels for 0%

commit v1 on v0

--- a/solution.py
+++ b/solution.py
@@ -52,7 +52,9 @@
     row_peak, row_total, weighted = attend_piece(
         fresh_state(row_count, head_count),
         query_heads,
-        lax.all_gather(key_vectors, "ctx", axis=0, tiled=True),
+        jnp.concatenate(
+            lax.all_to_all(jnp.stack([key_vectors] * lax.axis_size("ctx")), "ctx", 0, 0), axis=0
+        ),
         lax.all_gather(value_vectors, "ctx", axis=0, tiled=True),
         score_scale,
     )

time: 812 us -> 591 us (0.73)
  the two profiles are of different devices: /device:TPU:21 before, /device:TPU:17 now
where the time goes in v1:
time: 591 us; the launch traced here: 590 us
  waiting for transfers between devices  302 us (51%)
  blocking collectives  185 us (31%)
  local copies, waits for them, and re-layouts  46.8 us (8%)
  matrix products  21.7 us (4%)
  starting transfers between devices  15 us (3%)
  between operations  13.2 us (2%)
    all_gather x1, waiting for transfers between devices, local(): lax.all_gather(value_vectors, 'ctx', axis=0, tiled=True)  188 us
    all_gather x1, blocking collectives, local(): all_queries = lax.all_gather(query_vectors, 'tp', axis=0, tiled=True)  97.2 us
    all_to_all x1, waiting for transfers between devices, local(): lax.all_to_all(jnp.stack([key_vectors] * lax.axis_size('ctx')), 'ctx', 0, 0)  61.3 us
    pmax x1, blocking collectives, local(): top_peak = lax.pmax(row_peak, 'tp')  61 us
    reduce_scatter x1, waiting for transfers between devices, local(): lax.psum_scatter(jnp.dot(attended, out_weight, preferred_element_type=jnp...  41.7 us
    psum x1, blocking collectives, local(): all_totals = lax.psum(row_total * factor, 'tp')  27.2 us
    dynamic_slice x8, local copies, waits for them, and re-layouts, attend_piece(): finished, unused = lax.scan(absorb, running, (key_parts, value_parts))  26.1 us
    unnamed x5, local copies, waits for them, and re-layouts  16 us
  transfers between devices with their start and end apart: 4, of which 4 were waited for; matrix products, arithmetic and copies ran while one was open for 2% of the time, Pallas kernels for 0%

profile of v1, /device:TPU:17, one launch (start us, length us, event | category | flops | bytes accessed | tf_op | source)
XLA Modules:
  0.0 590.2 jit_solution(7567424278455338486)
XLA Ops:
  6.5 4.3 stack.2
  10.9 14.9 %all-to-all-start = ((bf16[64,16,3072]{2,1,0:T(8,128)(2,1)}), bf16[64,16,3072]{2,1,0:T(8,128)(2,1)}, u32[]{:S(2)}, u32[]{:S(2)}) async-start(bf16[64,16,3072]{2,1,0:T(8,128)(2,1)} %stack.2), calls=%async_computation | async-start | bytes 12582912 | tf_op jit(solution)/shard_map/all_to_all | solution.py:56
  25.8 0.7 all-gather.2.cloned.1.call-update
  26.6 97.2 %all_gather.6 = bf16[128,3072]{1,0:T(8,128)(2,1)S(1)} all-gather(bf16[16,3072]{1,0:T(8,128)(2,1)S(1)} %copy-done.1), channel_id=1, replica_groups=mesh['ctx'=64,'tp'=8] {'tp'}, dimensions={0}, use_global_device_ids=true | all-gather | bytes 884736 | tf_op jit(solution)/shard_map/all_gather | solution.py:48
  124.2 1.2 copy.14
  125.4 61.3 %all-to-all-done = bf16[64,16,3072]{2,1,0:T(8,128)(2,1)} async-done(((bf16[64,16,3072]{2,1,0:T(8,128)(2,1)}), bf16[64,16,3072]{2,1,0:T(8,128)(2,1)}, u32[]{:S(2)}, u32[]{:S(2)}) %all-to-all-start) | async-done | bytes 6291488 | tf_op jit(solution)/shard_map/all_to_all | solution.py:56
  186.7 7.4 %copy.19 = bf16[128,8,24,128]{3,2,1,0:T(8,128)(2,1)} copy(bf16[128,8,24,128]{3,1,2,0:T(8,128)(2,1)} %bitcast.8) | data formatting | bytes 12582912
  194.1 187.9 %all-gather.2.cloned.1.call-done = bf16[1024,3072]{1,0:T(8,128)(2,1)} async-done(((bf16[16,3072]{1,0:T(8,128)(2,1)}), bf16[1024,3072]{1,0:T(8,128)(2,1)}) %all-gather.2.cloned.1.call-update) | async-done | bytes 6291472 | tf_op jit(solution)/shard_map/all_gather | solution.py:58
  382.0 7.4 %copy.20 = bf16[128,8,24,128]{3,2,1,0:T(8,128)(2,1)} copy(bf16[128,8,24,128]{3,1,2,0:T(8,128)(2,1)} %bitcast.54) | data formatting | bytes 12582912
  389.3 46.2 %while.15 = (s32[]{:T(128)}, f32[128,24]{0,1:T(8,128)S(1)}, f32[128,24]{0,1:T(8,128)S(1)}, f32[128,24,128]{0,2,1:T(8,128)}, bf16[4,256,24,128]{3,2,1,0:T(8,128)(...) while((s32[]{:T(128)}, f32[128,24]{0,1:T(8,128)S(1)}, ...), condition=%wide.region_3.4_spmd.clone, body=%wide.region_0.3_spmd.clone.sunk | while | flops 411712512 | bytes 29294728 | solution.py:41
  389.3 3.6 constant_dynamic-slice_fusion.4
  393.0 0.6 bitcast_reduce_fusion.2
  394.2 2.9 copy.28
  397.1 3.5 bitcast_add_fusion.2
  400.5 3.6 constant_dynamic-slice_fusion.4
  404.2 0.6 bitcast_reduce_fusion.2
  405.4 2.9 copy.28
  408.3 3.9 bitcast_add_fusion.2
  412.2 3.6 constant_dynamic-slice_fusion.4
  415.9 0.6 bitcast_reduce_fusion.2
  417.0 2.9 copy.28
  419.9 3.9 bitcast_add_fusion.2
  423.9 3.6 constant_dynamic-slice_fusion.4
  428.7 2.9 copy.28
  431.6 3.9 bitcast_add_fusion.2
  435.6 61.0 %pmax.7 = f32[128,24]{0,1:T(8,128)S(1)} all-reduce(f32[128,24]{0,1:T(8,128)S(1)} %get-tuple-element.45), channel_id=1, replica_groups=mesh['ctx'=64,'tp'=8] {'tp'}, use_global_device_ids=true, to_apply=%region_4.5 | all-reduce | flops 3072 | bytes 24576 | tf_op jit(solution)/shard_map/pmax | solution.py:61
  496.6 2.5 multiply_convert_fusion
  499.2 27.2 %psum.7 = f32[128,24]{0,1:T(8,128)S(1)} all-reduce(f32[128,24]{0,1:T(8,128)S(1)} %get-tuple-element.101), channel_id=1, replica_groups=mesh['ctx'=64,'tp'=8] {'tp'}, use_global_device_ids=true, to_apply=%region_6.7 | all-reduce | flops 3072 | bytes 24576 | tf_op jit(solution)/shard_map/psum | solution.py:63
  526.4 10.6 %reduce-scatter.3.cloned.1.call-done = bf16[128,384]{0,1:T(8,128)(2,1)} async-done(((bf16[128,3072]{0,1:T(8,128)(2,1)}), bf16[128,384]{0,1:T(8,128)(2,1)}) %reduce-scatter.3.cloned.1.call-update) | async-done | bytes 98320 | tf_op jit(solution)/shard_map/reduce_scatter | solution.py:65
  537.0 0.9 fusion.10
  537.9 4.1 convolution_convert_fusion
  542.0 41.7 %reduce-scatter.5.cloned.1.call-done = bf16[16,5120]{1,0:T(8,128)(2,1)} async-done(((bf16[128,5120]{1,0:T(8,128)(2,1)}), bf16[16,5120]{1,0:T(8,128)(2,1)}) %reduce-scatter.5.cloned.1.call-update) | async-done | bytes 163856 | tf_op jit(solution)/shard_map/reduce_scatter | solution.py:76
  (38 shorter events, 3.4 us)
Async XLA Ops:
  10.9 15.7 %copy-start.1 = (bf16[16,3072]{1,0:T(8,128)(2,1)S(1)}, bf16[16,3072]{1,0:T(8,128)(2,1)}, u32[]{:S(2)}) copy-start(bf16[16,3072]{1,0:T(8,128)(2,1)} %param.6) | copy-start | bytes 294916
  10.9 175.8 %all-to-all-start = ((bf16[64,16,3072]{2,1,0:T(8,128)(2,1)}), bf16[64,16,3072]{2,1,0:T(8,128)(2,1)}, u32[]{:S(2)}, u32[]{:S(2)}) async-start(bf16[64,16,3072]{2,1,0:T(8,128)(2,1)} %stack.2), calls=%async_computation | async-start | bytes 12582912 | tf_op jit(solution)/shard_map/all_to_all | solution.py:56
  25.8 356.2 %all-gather.2.cloned.1.call-start = ((), (), s32[]{:S(2)}) async-start(), calls=%async_computation.3 | async-start | bytes 6389760 | tf_op jit(solution)/shard_map/all_gather | solution.py:58
  26.5 510.5 %reduce-scatter.3.cloned.1.call-start = ((), (), s32[]{:S(2)}) async-start(), calls=%async_computation.4 | async-start | bytes 884736 | tf_op jit(solution)/shard_map/reduce_scatter | solution.py:65
  389.3 3.6 copy-start
  400.5 3.6 copy-start
  412.2 3.6 copy-start
  423.9 3.6 copy-start
  499.1 84.5 %reduce-scatter.5.cloned.1.call-start = ((), (), s32[]{:S(2)}) async-start(), calls=%async_computation.5 | async-start | bytes 1474560 | tf_op jit(solution)/shard_map/reduce_scatter | solution.py:76
Sparse Core Ops, SparseCore 0:
  28.7 353.2 all-gather.1
  499.3 37.6 reduce-scatter.2
  542.1 41.5 reduce-scatter.4
